TPU v7x, 32 devices: a whole 2x2x4 slice. The times are simulated.
32 devices in a mesh: px: 4 (over x, core), py: 8 (over z, y).
Axes of the slice: x: 2, y: 2, z: 4, core: 2. Of those that a mesh axis runs over, the one named last changes fastest.
Arguments:
- fraction: float32 [32, 64, 640], P('px', 'py'), may hold values from 0 to 1
- courant_x: float32 [32, 64, 640], P('px', 'py'), may hold values from -0.5 to 0.5
- courant_y: float32 [32, 64, 640], P('px', 'py'), may hold values from -0.5 to 0.5
- courant_z: float32 [32, 64, 640], P('px', 'py'), may hold values from -0.5 to 0.5
- labels: int32 [32, 64, 640], P('px', 'py'), may hold values from -1 to 31, as said below
- structure_owner: int32 [4, 32], P('px'), may hold values from 0 to 7, as said below
- parcel_owner: int32 [4, 32], P('px'), may hold values from 0 to 7, as said below
Outputs:
- remaining: float32 [32, 64, 640], P('px', 'py')
- moments: float32 [4, 13, 32], P('px', None, 'py')
- parcels: float32 [4, 13, 32], P('px', None, 'py')
Inputs may be any that keep to these rules, and one draw needn't show every extreme that they name: `labels`: a label names a structure of the cell's row. `structure_owner`: in each row every index of py owns exactly 4 structures. `parcel_owner`: in each row every index of py receives exactly 4 parcels.
All inputs are finite; a program needn't handle non-finite values.
Results may differ from a plain program's by a relative error of at most 0.0003.
Values sent between devices are 32-bit elements; how exact they have to be, the bound alone decides.
A program may use at most 64 MiB of HBM per device.

v0:
```python
import math
import jax
import jax.numpy as jnp
from jax import lax
from jax.sharding import PartitionSpec as P


def with_halo(x, sides, width, wrap):
    for axis, dim in sides:
        size, length = (lax.axis_size(axis), x.shape[dim])
        up = [(i, (i + 1) % size) for i in range(size if wrap else size - 1)]
        down = [(j, i) for i, j in up]
        last = lax.slice_in_dim(x, length - width, length, axis=dim)
        initial = lax.slice_in_dim(x, 0, width, axis=dim)
        before = lax.ppermute(last, axis, up)
        after = lax.ppermute(initial, axis, down)
        x = jnp.concatenate([before, x, after], axis=dim)
    return x


def advance(padded_frac, padded_cour, length, axis):

    def part(array, start, count):
        return lax.slice_in_dim(array, start, start + count, axis=axis)

    centre = part(padded_frac, 1, length + 2)
    spread = 0.5 * (part(padded_frac, 2, length + 2) - part(padded_frac, 0, length + 2))
    bound = 2.0 * jnp.minimum(centre, 1.0 - centre)
    slope = jnp.minimum(jnp.maximum(spread, -bound), bound)
    courant = part(padded_cour, 1, length + 1)
    upwind = part(centre, 0, length + 1) + 0.5 * (1.0 - courant) * part(slope, 0, length + 1)
    downwind = part(centre, 1, length + 1) - 0.5 * (1.0 + courant) * part(slope, 1, length + 1)
    flux = courant * jnp.where(courant > 0.0, upwind, downwind)
    middle = part(padded_frac, 2, length)
    high = part(courant, 1, length)
    low = part(courant, 0, length)
    updated = middle - (part(flux, 1, length) - part(flux, 0, length)) + middle * (high - low)
    return (updated, 0.5 * (high + low))


def parcel_rows(moment_rows):
    volume = moment_rows[0]
    safe = jnp.maximum(volume, 0.5)
    centre = moment_rows[1:4] / safe
    velocity = moment_rows[4:7] / safe
    square = moment_rows[7:10] / safe - centre * centre
    cross = jnp.stack(
        [
            moment_rows[10] / safe - centre[0] * centre[1],
            moment_rows[11] / safe - centre[0] * centre[2],
            moment_rows[12] / safe - centre[1] * centre[2],
        ]
    )
    return jnp.concatenate([volume[None], centre, velocity, square, cross], 0)


def slot_table(owner_row, per_owner):
    count = owner_row.shape[0]
    index = jnp.arange(count, dtype=jnp.int32)
    same = owner_row[:, None] == owner_row[None, :]
    earlier = index[None, :] < index[:, None]
    rank = jnp.sum((same & earlier).astype(jnp.int32), axis=1)
    position = owner_row * per_owner + rank
    return (position[:, None] == index[None, :]).astype(jnp.float32)


def product(left, right):
    return jnp.dot(left, right, precision=lax.Precision.HIGHEST, preferred_element_type=jnp.float32)


def local(fraction, courant_x, courant_y, courant_z, labels, structure_owner, parcel_owner):
    rows_x, rows_y, depth = fraction.shape
    padded = with_halo(jnp.stack([fraction, courant_x]), (("px", 1),), 2, True)
    first, velocity_x = advance(padded[0], padded[1], rows_x, 0)
    padded_y = with_halo(jnp.stack([first, courant_y]), (("py", 2),), 2, False)
    second, velocity_y = advance(padded_y[0], padded_y[1], rows_y, 1)
    pad_z = ((0, 0), (0, 0), (2, 2))
    third, velocity_z = advance(jnp.pad(second, pad_z), jnp.pad(courant_z, pad_z), depth, 2)
    remaining = jnp.where(labels >= 0, jnp.float32(0.0), third)
    width_py = lax.axis_size("py")
    row_index = lax.axis_index("py")
    total_x = rows_x * lax.axis_size("px")
    total_y = rows_y * width_py
    structures = structure_owner.shape[1]
    per_owner = structures // width_py
    scale = 4.0 / (rows_x * rows_y * rows_y)
    start_x = lax.axis_index("px") * rows_x
    start_y = row_index * rows_y
    coord_x = ((start_x + jnp.arange(rows_x, dtype=jnp.int32)).astype(jnp.float32) + 0.5)[
        :, None, None
    ] / total_x
    coord_y = ((start_y + jnp.arange(rows_y, dtype=jnp.int32)).astype(jnp.float32) + 0.5)[
        None, :, None
    ] / total_y
    coord_z = (jnp.arange(depth, dtype=jnp.int32).astype(jnp.float32) + 0.5)[None, None, :] / depth
    weight = third * scale
    shape = weight.shape
    cells = rows_x * rows_y * depth
    block = math.gcd(cells, 4096)
    blocks = cells // block
    pieces = [
        jnp.ones(shape, jnp.float32),
        coord_x,
        coord_y,
        coord_z,
        velocity_x,
        velocity_y,
        velocity_z,
        coord_x * coord_x,
        coord_y * coord_y,
        coord_z * coord_z,
        coord_x * coord_y,
        coord_x * coord_z,
        coord_y * coord_z,
    ]
    feature_blocks = jnp.stack(
        [(weight * jnp.broadcast_to(piece, shape)).reshape(blocks, block) for piece in pieces], 1
    )
    label_blocks = labels.reshape(blocks, block)
    columns = jnp.arange(structures, dtype=jnp.int32)

    def accumulate(total, inputs):
        feature_rows, marks = inputs
        onehot = (marks[:, None] == columns[None, :]).astype(jnp.float32)
        return (total + product(feature_rows, onehot), None)

    partial_sums, unused = lax.scan(
        accumulate, jnp.zeros((13, structures), jnp.float32), (feature_blocks, label_blocks)
    )
    owner_slots = slot_table(structure_owner[0], per_owner)
    parcel_slots = slot_table(parcel_owner[0], per_owner)
    mine_owned = lax.dynamic_slice_in_dim(owner_slots, row_index * per_owner, per_owner, 1)
    totals = lax.psum(partial_sums, "py")
    owned = product(totals, mine_owned)
    mine_parcels = lax.dynamic_slice_in_dim(parcel_slots, row_index * per_owner, per_owner, 1)
    received = product(parcel_rows(totals), mine_parcels)
    return (remaining, owned[None], received[None])


def solution(mesh):
    return jax.shard_map(
        local,
        mesh=mesh,
        in_specs=(
            P("px", "py", None),
            P("px", "py", None),
            P("px", "py", None),
            P("px", "py", None),
            P("px", "py", None),
            P("px", None),
            P("px", None),
        ),
        out_specs=(P("px", "py", None), P("px", None, "py"), P("px", None, "py")),
        check_vma=False,
    )
```

profile of v0, /device:TPU:0, one launch (start us, length us, event | category | flops | bytes accessed | tf_op | source)
XLA Modules:
  0.0 86.4 jit_solution(18232538209815463961)
XLA Ops:
  1.6 2.5 %collective-permute-start.1 = (f32[2,2,8,640]{3,2,1,0:T(8,128)S(1)}, f32[2,2,8,640]{3,2,1,0:T(8,128)S(1)}, u32[]{:S(2)}, u32[]{:S(2)}) collective-permute-start(f32[2,2,8,640]{3,2,1,0:T(8,128)S(1)} %get-tuple-element.72), channel_id=1, source_target_pairs={{8,0},{16,8},{24,16},{0,24},{9,1},{17,9},{25,17},{1,25},{10,2},{18... | collective-permute-start | bytes 245768 | tf_op jit(solution)/shard_map/ppermute | solution.py:16
  4.2 1.7 %reshape.154 = s32[10,4096]{1,0:T(8,128)} reshape(s32[8,8,640]{2,1,0:T(8,128)} %param.13) | data formatting | bytes 327680 | tf_op jit(solution)/shard_map/reshape | solution.py:119
  5.9 0.9 %convert_reduce_fusion = s32[32]{0:T(128)S(1)} fusion(s32[32]{0:T(128)} %bitcast.70), kind=kLoop, calls=%fused_computation.112 | loop fusion | flops 5088 | bytes 256 | tf_op jit(solution)/shard_map/reduce_sum | solution.py:62
  7.5 0.9 %convert_reduce_fusion.1 = s32[32]{0:T(128)S(1)} fusion(s32[32]{0:T(128)} %bitcast.71), kind=kLoop, calls=%fused_computation.113 | loop fusion | flops 5088 | bytes 256 | tf_op jit(solution)/shard_map/reduce_sum | solution.py:62
  9.0 1.2 %pad_maximum_fusion.1 = (f32[2,10,8,640]{3,2,1,0:T(8,128)S(1)}, f32[2,10,8,640]{3,2,1,0:T(8,128)S(1)}) fusion(f32[2,2,8,640]{3,2,1,0:T(8,128)S(1)} %collective-permute-done.1, f32[1,8,8,640]{3,2,1,0:T(8,128)} %bitcast.60, f32[1,8,8,640]{3,2,1,0:T(8,128)} %bitcast.64, f32[2,2,8,640]{3,2,1,0:T(8,128)S(1)} %collective-permute-done), kind=kLoop, calls=%fused_computation.12 | loop fusion | flops 409600 | bytes 1310720 | tf_op jit(solution)/shard_map/concatenate | solution.py:17
  10.3 1.0 %fusion.16 = f32[10,8,640]{2,1,0:T(8,128)S(1)} fusion(f32[2,10,8,640]{3,2,1,0:T(8,128)S(1)} %get-tuple-element.71, f32[2,10,8,640]{3,2,1,0:T(8,128)S(1)} %get-tuple-element.70, f32[2,2,8,640]{3,2,1,0:T(8,128)S(1)} %collective-permute-done.1, f32[1,8,8,640]{3,2,1,0:T(8,128)} %bitcast.61, f32[1,8,8,640]{3,2,1,0:T(8,128)} %bitcast.65, ...), kind=kLoop, calls=%fused_computation.42 | loop fusion | flops 563200 | bytes 1105920 | tf_op jit(solution)/shard_map/min | solution.py:29
  11.5 3.4 %collective-permute-start.2 = (f32[2,8,2,640]{3,2,1,0:T(2,128)S(1)}, f32[2,8,2,640]{3,2,1,0:T(2,128)S(1)}, u32[]{:S(2)}, u32[]{:S(2)}) collective-permute-start(f32[2,8,2,640]{3,2,1,0:T(2,128)S(1)} %get-tuple-element.68), channel_id=1, source_target_pairs={{0,1},{1,2},{2,3},{3,4},{4,5},{5,6},{6,7},{8,9},{9,10},{10,11},{11... | collective-permute-start | bytes 245768 | tf_op jit(solution)/shard_map/ppermute | solution.py:15
  14.9 1.3 %collective-permute-start.3 = (f32[2,8,2,640]{3,2,1,0:T(2,128)S(1)}, f32[2,8,2,640]{3,2,1,0:T(2,128)S(1)}, u32[]{:S(2)}, u32[]{:S(2)}) collective-permute-start(f32[2,8,2,640]{3,2,1,0:T(2,128)S(1)} %get-tuple-element.69), channel_id=1, source_target_pairs={{1,0},{2,1},{3,2},{4,3},{5,4},{6,5},{7,6},{9,8},{10,9},{11,10},{12... | collective-permute-start | bytes 245768 | tf_op jit(solution)/shard_map/ppermute | solution.py:16
  16.2 1.3 %collective-permute-done.2 = f32[2,8,2,640]{3,2,1,0:T(2,128)S(1)} collective-permute-done((f32[2,8,2,640]{3,2,1,0:T(2,128)S(1)}, f32[2,8,2,640]{3,2,1,0:T(2,128)S(1)}, u32[]{:S(2)}, u32[]{:S(2)}) %collective-permute-start.2) | collective-permute-done | bytes 81952 | tf_op jit(solution)/shard_map/ppermute | solution.py:15
  17.5 4.1 %collective-permute-done.3 = f32[2,8,2,640]{3,2,1,0:T(2,128)S(1)} collective-permute-done((f32[2,8,2,640]{3,2,1,0:T(2,128)S(1)}, f32[2,8,2,640]{3,2,1,0:T(2,128)S(1)}, u32[]{:S(2)}, u32[]{:S(2)}) %collective-permute-start.3) | collective-permute-done | bytes 81952 | tf_op jit(solution)/shard_map/ppermute | solution.py:16
  33.7 30.6 %while.11 = (s32[]{:T(128)}, f32[13,32]{1,0:T(8,128)S(1)}, f32[10,13,4096]{2,0,1:T(8,128)}, s32[10,4096]{1,0:T(8,128)}, s32[]{:T(128)}, /*index=5*/s32[]{:T(128)}) while((s32[]{:T(128)}, f32[13,32]{1,0:T(8,128)S(1)}, f32[10,13,4096]{2,0,1:T(8,128)}, s32[10,4096]{1,0:T(8,128)}, s32[]{:T(128)}, /*index=5*/s32[]{:T(128)}) %tuple.55), condition=%wide.region_1.2_spmd.clone, body=%wide.region_0.1_spmd.clone.sunk | while | flops 20579140 | bytes 691543 | solution.py:127
  33.7 1.6 %constant_dynamic-slice_fusion.4 = f32[1,13,4096]{2,0,1:T(1,128)S(1)} fusion(f32[10,13,4096]{2,0,1:T(8,128)} %get-tuple-element.143, s32[]{:T(128)} %get-tuple-element.135), kind=kLoop, calls=%fused_computation.6.clone.1 | loop fusion | bytes 425988 | tf_op jit(solution)/shard_map/while/body/jit(dynamic_index_in_dim)/dynamic_slice | solution.py:127
  35.4 0.9 %constant_dynamic-slice_fusion.5 = s32[1,4096]{1,0:T(1,128)S(1)} fusion(s32[10,4096]{1,0:T(8,128)} %get-tuple-element.144, s32[]{:T(128)} %get-tuple-element.135), kind=kLoop, calls=%fused_computation.5.clone.1 | loop fusion | bytes 32772 | tf_op jit(solution)/shard_map/while/body/jit(dynamic_index_in_dim)/dynamic_slice | solution.py:127
  36.8 1.6 %constant_dynamic-slice_fusion.4 = f32[1,13,4096]{2,0,1:T(1,128)S(1)} fusion(f32[10,13,4096]{2,0,1:T(8,128)} %get-tuple-element.143, s32[]{:T(128)} %get-tuple-element.135), kind=kLoop, calls=%fused_computation.6.clone.1 | loop fusion | bytes 425988 | tf_op jit(solution)/shard_map/while/body/jit(dynamic_index_in_dim)/dynamic_slice | solution.py:127
  38.5 0.9 %constant_dynamic-slice_fusion.5 = s32[1,4096]{1,0:T(1,128)S(1)} fusion(s32[10,4096]{1,0:T(8,128)} %get-tuple-element.144, s32[]{:T(128)} %get-tuple-element.135), kind=kLoop, calls=%fused_computation.5.clone.1 | loop fusion | bytes 32772 | tf_op jit(solution)/shard_map/while/body/jit(dynamic_index_in_dim)/dynamic_slice | solution.py:127
  39.9 1.6 %constant_dynamic-slice_fusion.4 = f32[1,13,4096]{2,0,1:T(1,128)S(1)} fusion(f32[10,13,4096]{2,0,1:T(8,128)} %get-tuple-element.143, s32[]{:T(128)} %get-tuple-element.135), kind=kLoop, calls=%fused_computation.6.clone.1 | loop fusion | bytes 425988 | tf_op jit(solution)/shard_map/while/body/jit(dynamic_index_in_dim)/dynamic_slice | solution.py:127
  41.5 0.9 %constant_dynamic-slice_fusion.5 = s32[1,4096]{1,0:T(1,128)S(1)} fusion(s32[10,4096]{1,0:T(8,128)} %get-tuple-element.144, s32[]{:T(128)} %get-tuple-element.135), kind=kLoop, calls=%fused_computation.5.clone.1 | loop fusion | bytes 32772 | tf_op jit(solution)/shard_map/while/body/jit(dynamic_index_in_dim)/dynamic_slice | solution.py:127
  42.9 1.6 %constant_dynamic-slice_fusion.4 = f32[1,13,4096]{2,0,1:T(1,128)S(1)} fusion(f32[10,13,4096]{2,0,1:T(8,128)} %get-tuple-element.143, s32[]{:T(128)} %get-tuple-element.135), kind=kLoop, calls=%fused_computation.6.clone.1 | loop fusion | bytes 425988 | tf_op jit(solution)/shard_map/while/body/jit(dynamic_index_in_dim)/dynamic_slice | solution.py:127
  44.6 0.9 %constant_dynamic-slice_fusion.5 = s32[1,4096]{1,0:T(1,128)S(1)} fusion(s32[10,4096]{1,0:T(8,128)} %get-tuple-element.144, s32[]{:T(128)} %get-tuple-element.135), kind=kLoop, calls=%fused_computation.5.clone.1 | loop fusion | bytes 32772 | tf_op jit(solution)/shard_map/while/body/jit(dynamic_index_in_dim)/dynamic_slice | solution.py:127
  46.0 1.6 %constant_dynamic-slice_fusion.4 = f32[1,13,4096]{2,0,1:T(1,128)S(1)} fusion(f32[10,13,4096]{2,0,1:T(8,128)} %get-tuple-element.143, s32[]{:T(128)} %get-tuple-element.135), kind=kLoop, calls=%fused_computation.6.clone.1 | loop fusion | bytes 425988 | tf_op jit(solution)/shard_map/while/body/jit(dynamic_index_in_dim)/dynamic_slice | solution.py:127
  47.7 0.9 %constant_dynamic-slice_fusion.5 = s32[1,4096]{1,0:T(1,128)S(1)} fusion(s32[10,4096]{1,0:T(8,128)} %get-tuple-element.144, s32[]{:T(128)} %get-tuple-element.135), kind=kLoop, calls=%fused_computation.5.clone.1 | loop fusion | bytes 32772 | tf_op jit(solution)/shard_map/while/body/jit(dynamic_index_in_dim)/dynamic_slice | solution.py:127
  49.1 1.6 %constant_dynamic-slice_fusion.4 = f32[1,13,4096]{2,0,1:T(1,128)S(1)} fusion(f32[10,13,4096]{2,0,1:T(8,128)} %get-tuple-element.143, s32[]{:T(128)} %get-tuple-element.135), kind=kLoop, calls=%fused_computation.6.clone.1 | loop fusion | bytes 425988 | tf_op jit(solution)/shard_map/while/body/jit(dynamic_index_in_dim)/dynamic_slice | solution.py:127
  50.7 0.9 %constant_dynamic-slice_fusion.5 = s32[1,4096]{1,0:T(1,128)S(1)} fusion(s32[10,4096]{1,0:T(8,128)} %get-tuple-element.144, s32[]{:T(128)} %get-tuple-element.135), kind=kLoop, calls=%fused_computation.5.clone.1 | loop fusion | bytes 32772 | tf_op jit(solution)/shard_map/while/body/jit(dynamic_index_in_dim)/dynamic_slice | solution.py:127
  52.1 1.6 %constant_dynamic-slice_fusion.4 = f32[1,13,4096]{2,0,1:T(1,128)S(1)} fusion(f32[10,13,4096]{2,0,1:T(8,128)} %get-tuple-element.143, s32[]{:T(128)} %get-tuple-element.135), kind=kLoop, calls=%fused_computation.6.clone.1 | loop fusion | bytes 425988 | tf_op jit(solution)/shard_map/while/body/jit(dynamic_index_in_dim)/dynamic_slice | solution.py:127
  53.8 0.9 %constant_dynamic-slice_fusion.5 = s32[1,4096]{1,0:T(1,128)S(1)} fusion(s32[10,4096]{1,0:T(8,128)} %get-tuple-element.144, s32[]{:T(128)} %get-tuple-element.135), kind=kLoop, calls=%fused_computation.5.clone.1 | loop fusion | bytes 32772 | tf_op jit(solution)/shard_map/while/body/jit(dynamic_index_in_dim)/dynamic_slice | solution.py:127
  55.2 1.6 %constant_dynamic-slice_fusion.4 = f32[1,13,4096]{2,0,1:T(1,128)S(1)} fusion(f32[10,13,4096]{2,0,1:T(8,128)} %get-tuple-element.143, s32[]{:T(128)} %get-tuple-element.135), kind=kLoop, calls=%fused_computation.6.clone.1 | loop fusion | bytes 425988 | tf_op jit(solution)/shard_map/while/body/jit(dynamic_index_in_dim)/dynamic_slice | solution.py:127
  56.9 0.9 %constant_dynamic-slice_fusion.5 = s32[1,4096]{1,0:T(1,128)S(1)} fusion(s32[10,4096]{1,0:T(8,128)} %get-tuple-element.144, s32[]{:T(128)} %get-tuple-element.135), kind=kLoop, calls=%fused_computation.5.clone.1 | loop fusion | bytes 32772 | tf_op jit(solution)/shard_map/while/body/jit(dynamic_index_in_dim)/dynamic_slice | solution.py:127
  58.3 1.6 %constant_dynamic-slice_fusion.4 = f32[1,13,4096]{2,0,1:T(1,128)S(1)} fusion(f32[10,13,4096]{2,0,1:T(8,128)} %get-tuple-element.143, s32[]{:T(128)} %get-tuple-element.135), kind=kLoop, calls=%fused_computation.6.clone.1 | loop fusion | bytes 425988 | tf_op jit(solution)/shard_map/while/body/jit(dynamic_index_in_dim)/dynamic_slice | solution.py:127
  59.9 0.9 %constant_dynamic-slice_fusion.5 = s32[1,4096]{1,0:T(1,128)S(1)} fusion(s32[10,4096]{1,0:T(8,128)} %get-tuple-element.144, s32[]{:T(128)} %get-tuple-element.135), kind=kLoop, calls=%fused_computation.5.clone.1 | loop fusion | bytes 32772 | tf_op jit(solution)/shard_map/while/body/jit(dynamic_index_in_dim)/dynamic_slice | solution.py:127
  61.3 1.6 %constant_dynamic-slice_fusion.4 = f32[1,13,4096]{2,0,1:T(1,128)S(1)} fusion(f32[10,13,4096]{2,0,1:T(8,128)} %get-tuple-element.143, s32[]{:T(128)} %get-tuple-element.135), kind=kLoop, calls=%fused_computation.6.clone.1 | loop fusion | bytes 425988 | tf_op jit(solution)/shard_map/while/body/jit(dynamic_index_in_dim)/dynamic_slice | solution.py:127
  63.0 0.9 %constant_dynamic-slice_fusion.5 = s32[1,4096]{1,0:T(1,128)S(1)} fusion(s32[10,4096]{1,0:T(8,128)} %get-tuple-element.144, s32[]{:T(128)} %get-tuple-element.135), kind=kLoop, calls=%fused_computation.5.clone.1 | loop fusion | bytes 32772 | tf_op jit(solution)/shard_map/while/body/jit(dynamic_index_in_dim)/dynamic_slice | solution.py:127
  64.4 20.1 %psum.7 = f32[13,32]{1,0:T(8,128)S(1)} all-reduce(f32[13,32]{1,0:T(8,128)S(1)} %get-tuple-element.30), channel_id=1, replica_groups=mesh['px'=4,'py'=8] {'py'}, use_global_device_ids=true, to_apply=%region_2.3 | all-reduce | flops 416 | bytes 3328 | tf_op jit(solution)/shard_map/psum | solution.py:133
  (78 shorter events, 21.0 us)
Async XLA Ops:
  0.6 10.6 %copy-start.1 = (f32[8,8,640]{2,1,0:T(8,128)S(1)}, f32[8,8,640]{2,1,0:T(8,128)}, u32[]{:S(2)}) copy-start(f32[8,8,640]{2,1,0:T(8,128)} %param.9) | copy-start | bytes 491524
  0.6 10.6 %copy-start = (f32[8,8,640]{2,1,0:T(8,128)S(1)}, f32[8,8,640]{2,1,0:T(8,128)}, u32[]{:S(2)}) copy-start(f32[8,8,640]{2,1,0:T(8,128)} %param.10) | copy-start | bytes 491524
  0.7 10.8 %copy-start.4 = (f32[8,8,640]{2,1,0:T(8,128)S(1)}, f32[8,8,640]{2,1,0:T(8,128)}, u32[]{:S(2)}) copy-start(f32[8,8,640]{2,1,0:T(8,128)} %param.11) | copy-start | bytes 491524
  1.6 7.5 %collective-permute-start.1 = (f32[2,2,8,640]{3,2,1,0:T(8,128)S(1)}, f32[2,2,8,640]{3,2,1,0:T(8,128)S(1)}, u32[]{:S(2)}, u32[]{:S(2)}) collective-permute-start(f32[2,2,8,640]{3,2,1,0:T(8,128)S(1)} %get-tuple-element.72), channel_id=1, source_target_pairs={{8,0},{16,8},{24,16},{0,24},{9,1},{17,9},{25,17},{1,25},{10,2},{18... | collective-permute-start | bytes 245768 | tf_op jit(solution)/shard_map/ppermute | solution.py:16
  4.0 5.0 %collective-permute-start = (f32[2,2,8,640]{3,2,1,0:T(8,128)S(1)}, f32[2,2,8,640]{3,2,1,0:T(8,128)S(1)}, u32[]{:S(2)}, u32[]{:S(2)}) collective-permute-start(f32[2,2,8,640]{3,2,1,0:T(8,128)S(1)} %get-tuple-element.73), channel_id=1, source_target_pairs={{0,8},{8,16},{16,24},{24,0},{1,9},{9,17},{17,25},{25,1},{2,10},{10... | collective-permute-start | bytes 245768 | tf_op jit(solution)/shard_map/ppermute | solution.py:15
  11.5 6.0 %collective-permute-start.2 = (f32[2,8,2,640]{3,2,1,0:T(2,128)S(1)}, f32[2,8,2,640]{3,2,1,0:T(2,128)S(1)}, u32[]{:S(2)}, u32[]{:S(2)}) collective-permute-start(f32[2,8,2,640]{3,2,1,0:T(2,128)S(1)} %get-tuple-element.68), channel_id=1, source_target_pairs={{0,1},{1,2},{2,3},{3,4},{4,5},{5,6},{6,7},{8,9},{9,10},{10,11},{11... | collective-permute-start | bytes 245768 | tf_op jit(solution)/shard_map/ppermute | solution.py:15
  14.9 6.7 %collective-permute-start.3 = (f32[2,8,2,640]{3,2,1,0:T(2,128)S(1)}, f32[2,8,2,640]{3,2,1,0:T(2,128)S(1)}, u32[]{:S(2)}, u32[]{:S(2)}) collective-permute-start(f32[2,8,2,640]{3,2,1,0:T(2,128)S(1)} %get-tuple-element.69), channel_id=1, source_target_pairs={{1,0},{2,1},{3,2},{4,3},{5,4},{6,5},{7,6},{9,8},{10,9},{11,10},{12... | collective-permute-start | bytes 245768 | tf_op jit(solution)/shard_map/ppermute | solution.py:16
  16.2 6.2 %copy-start.2 = (f32[8,8,640]{2,1,0:T(8,128)S(1)}, f32[8,8,640]{2,1,0:T(8,128)}, u32[]{:S(2)}) copy-start(f32[8,8,640]{2,1,0:T(8,128)} %param.12) | copy-start | bytes 491524
  21.8 1.0 %copy-start.3 = (s32[8,8,640]{2,1,0:T(8,128)S(1)}, s32[8,8,640]{2,1,0:T(8,128)}, u32[]{:S(2)}) copy-start(s32[8,8,640]{2,1,0:T(8,128)} %param.13) | copy-start | bytes 491524
where the time goes:
time: 87.1 us; the launch traced here: 86.4 us
  local copies, waits for them, and re-layouts  37.5 us (43%)
  blocking collectives  20.1 us (23%)
  other arithmetic  8.61 us (10%)
  starting transfers between devices  7.18 us (8%)
  matrix products  6.3 us (7%)
  waiting for transfers between devices  5.37 us (6%)
  between operations  0.97 us (1%)
    dynamic_slice x20, local copies, waits for them, and re-layouts, local(): lax.scan(accumulate, jnp.zeros((13, structures), jnp.float32), (feature_b...  25.7 us
    psum x1, blocking collectives, local(): totals = lax.psum(partial_sums, 'py')  20.1 us
    unnamed x22, local copies, waits for them, and re-layouts  8.8 us
    dot_general x12, matrix products, product(): jnp.dot(left, right, precision=lax.Precision.HIGHEST, preferred_element_t...  6.3 us
    ppermute x2, waiting for transfers between devices, with_halo(): after = lax.ppermute(initial, axis, down)  4.12 us
    ppermute x2, starting transfers between devices, with_halo(): after = lax.ppermute(initial, axis, down)  3.75 us
    ppermute x2, starting transfers between devices, with_halo(): before = lax.ppermute(last, axis, up)  3.43 us
    reduce_sum x2, other arithmetic, slot_table(): rank = jnp.sum((same & earlier).astype(jnp.int32), axis=1)  1.82 us
  transfers between devices with their start and end apart: 4, of which 2 were waited for; matrix products, arithmetic and copies ran while one was open for 6% of the time, Pallas kernels for 0%

commit v1 on v0

--- a/solution.py
+++ b/solution.py
@@ -130,7 +130,7 @@
     owner_slots = slot_table(structure_owner[0], per_owner)
     parcel_slots = slot_table(parcel_owner[0], per_owner)
     mine_owned = lax.dynamic_slice_in_dim(owner_slots, row_index * per_owner, per_owner, 1)
-    totals = lax.psum(partial_sums, "py")
+    totals = jnp.sum(lax.all_gather(partial_sums, "py"), axis=0)
     owned = product(totals, mine_owned)
     mine_parcels = lax.dynamic_slice_in_dim(parcel_slots, row_index * per_owner, per_owner, 1)
     received = product(parcel_rows(totals), mine_parcels)

time: 87.1 us -> 97.9 us (1.12)
  blocking collectives: 20.1 us -> 30.9 us
    all_gather x0 -> x1, blocking collectives: none -> 30.9 us  [local(): totals = jnp.sum(lax.all_gather(partial_sums, 'py'), axis=0)]
    psum x1 -> x0, blocking collectives: 20.1 us -> none  [local(): totals = lax.psum(partial_sums, 'py')]
  transfers between devices with their start and end apart: 4 -> 4, of which waited for: 2 -> 2; matrix products, arithmetic and copies ran while one was open for 6% -> 5% of each run, Pallas kernels for 0% -> 0%
where the time goes in v1:
time: 97.9 us; the launch traced here: 97.1 us
  local copies, waits for them, and re-layouts  37.5 us (38%)
  blocking collectives  30.9 us (32%)
  other arithmetic  8.62 us (9%)
  starting transfers between devices  7.18 us (7%)
  matrix products  6.3 us (6%)
  waiting for transfers between devices  5.37 us (5%)
    all_gather x1, blocking collectives, local(): totals = jnp.sum(lax.all_gather(partial_sums, 'py'), axis=0)  30.9 us
    dynamic_slice x20, local copies, waits for them, and re-layouts, local(): lax.scan(accumulate, jnp.zeros((13, structures), jnp.float32), (feature_b...  25.7 us
    unnamed x22, local copies, waits for them, and re-layouts  8.8 us
    dot_general x12, matrix products, product(): jnp.dot(left, right, precision=lax.Precision.HIGHEST, preferred_element_t...  6.3 us
    ppermute x2, waiting for transfers between devices, with_halo(): after = lax.ppermute(initial, axis, down)  4.12 us
    ppermute x2, starting transfers between devices, with_halo(): after = lax.ppermute(initial, axis, down)  3.75 us
    ppermute x2, starting transfers between devices, with_halo(): before = lax.ppermute(last, axis, up)  3.43 us
  transfers between devices with their start and end apart: 4, of which 2 were waited for; matrix products, arithmetic and copies ran while one was open for 5% of the time, Pallas kernels for 0%

profile of v1, /device:TPU:0, one launch (start us, length us, event | category | flops | bytes accessed | tf_op | source)
XLA Modules:
  0.0 97.1 jit_solution(156089805139490663)
XLA Ops:
  1.6 2.5 %collective-permute-start.1 = (f32[2,2,8,640]{3,2,1,0:T(8,128)S(1)}, f32[2,2,8,640]{3,2,1,0:T(8,128)S(1)}, u32[]{:S(2)}, u32[]{:S(2)}) collective-permute-start(f32[2,2,8,640]{3,2,1,0:T(8,128)S(1)} %get-tuple-element.76), channel_id=1, source_target_pairs={{8,0},{16,8},{24,16},{0,24},{9,1},{17,9},{25,17},{1,25},{10,2},{18... | collective-permute-start | bytes 245768 | tf_op jit(solution)/shard_map/ppermute | solution.py:16
  4.2 1.7 %reshape.154 = s32[10,4096]{1,0:T(8,128)} reshape(s32[8,8,640]{2,1,0:T(8,128)} %param.13) | data formatting | bytes 327680 | tf_op jit(solution)/shard_map/reshape | solution.py:119
  5.9 0.9 convert_reduce_fusion
  7.5 0.9 convert_reduce_fusion.1
  9.0 1.2 %pad_maximum_fusion.1 = (f32[2,10,8,640]{3,2,1,0:T(8,128)S(1)}, f32[2,10,8,640]{3,2,1,0:T(8,128)S(1)}) fusion(f32[2,2,8,640]{3,2,1,0:T(8,128)S(1)} %collective-permute-done.1, f32[1,8,8,640]{3,2,1,0:T(8,128)} %bitcast.61, f32[1,8,8,640]{3,2,1,0:T(8,128)} %bitcast.65, f32[2,2,8,640]{3,2,1,0:T(8,128)S(1)} %collective-permute-done), kind=kLoop, calls=%fused_computation.12 | loop fusion | flops 409600 | bytes 1310720 | tf_op jit(solution)/shard_map/concatenate | solution.py:17
  10.3 1.0 %fusion.16 = f32[10,8,640]{2,1,0:T(8,128)S(1)} fusion(f32[2,10,8,640]{3,2,1,0:T(8,128)S(1)} %get-tuple-element.75, f32[2,10,8,640]{3,2,1,0:T(8,128)S(1)} %get-tuple-element.74, f32[2,2,8,640]{3,2,1,0:T(8,128)S(1)} %collective-permute-done.1, f32[1,8,8,640]{3,2,1,0:T(8,128)} %bitcast.62, f32[1,8,8,640]{3,2,1,0:T(8,128)} %bitcast.66, ...), kind=kLoop, calls=%fused_computation.42 | loop fusion | flops 563200 | bytes 1105920 | tf_op jit(solution)/shard_map/min | solution.py:29
  11.5 3.4 %collective-permute-start.2 = (f32[2,8,2,640]{3,2,1,0:T(2,128)S(1)}, f32[2,8,2,640]{3,2,1,0:T(2,128)S(1)}, u32[]{:S(2)}, u32[]{:S(2)}) collective-permute-start(f32[2,8,2,640]{3,2,1,0:T(2,128)S(1)} %get-tuple-element.72), channel_id=1, source_target_pairs={{0,1},{1,2},{2,3},{3,4},{4,5},{5,6},{6,7},{8,9},{9,10},{10,11},{11... | collective-permute-start | bytes 245768 | tf_op jit(solution)/shard_map/ppermute | solution.py:15
  14.9 1.3 %collective-permute-start.3 = (f32[2,8,2,640]{3,2,1,0:T(2,128)S(1)}, f32[2,8,2,640]{3,2,1,0:T(2,128)S(1)}, u32[]{:S(2)}, u32[]{:S(2)}) collective-permute-start(f32[2,8,2,640]{3,2,1,0:T(2,128)S(1)} %get-tuple-element.73), channel_id=1, source_target_pairs={{1,0},{2,1},{3,2},{4,3},{5,4},{6,5},{7,6},{9,8},{10,9},{11,10},{12... | collective-permute-start | bytes 245768 | tf_op jit(solution)/shard_map/ppermute | solution.py:16
  16.2 1.3 %collective-permute-done.2 = f32[2,8,2,640]{3,2,1,0:T(2,128)S(1)} collective-permute-done((f32[2,8,2,640]{3,2,1,0:T(2,128)S(1)}, f32[2,8,2,640]{3,2,1,0:T(2,128)S(1)}, u32[]{:S(2)}, u32[]{:S(2)}) %collective-permute-start.2) | collective-permute-done | bytes 81952 | tf_op jit(solution)/shard_map/ppermute | solution.py:15
  17.5 4.1 %collective-permute-done.3 = f32[2,8,2,640]{3,2,1,0:T(2,128)S(1)} collective-permute-done((f32[2,8,2,640]{3,2,1,0:T(2,128)S(1)}, f32[2,8,2,640]{3,2,1,0:T(2,128)S(1)}, u32[]{:S(2)}, u32[]{:S(2)}) %collective-permute-start.3) | collective-permute-done | bytes 81952 | tf_op jit(solution)/shard_map/ppermute | solution.py:16
  33.7 30.6 %while.11 = (s32[]{:T(128)}, f32[13,32]{1,0:T(8,128)S(1)}, f32[10,13,4096]{2,0,1:T(8,128)}, s32[10,4096]{1,0:T(8,128)}, s32[]{:T(128)}, /*index=5*/s32[]{:T(128)}) while((s32[]{:T(128)}, f32[13,32]{1,0:T(8,128)S(1)}, f32[10,13,4096]{2,0,1:T(8,128)}, s32[10,4096]{1,0:T(8,128)}, s32[]{:T(128)}, /*index=5*/s32[]{:T(128)}) %tuple.56), condition=%wide.region_1.2_spmd.clone, body=%wide.region_0.1_spmd.clone.sunk | while | flops 20579140 | bytes 691543 | solution.py:127
  33.7 1.6 %constant_dynamic-slice_fusion.4 = f32[1,13,4096]{2,0,1:T(1,128)S(1)} fusion(f32[10,13,4096]{2,0,1:T(8,128)} %get-tuple-element.147, s32[]{:T(128)} %get-tuple-element.139), kind=kLoop, calls=%fused_computation.6.clone.1 | loop fusion | bytes 425988 | tf_op jit(solution)/shard_map/while/body/jit(dynamic_index_in_dim)/dynamic_slice | solution.py:127
  35.4 0.9 constant_dynamic-slice_fusion.5
  36.8 1.6 %constant_dynamic-slice_fusion.4 = f32[1,13,4096]{2,0,1:T(1,128)S(1)} fusion(f32[10,13,4096]{2,0,1:T(8,128)} %get-tuple-element.147, s32[]{:T(128)} %get-tuple-element.139), kind=kLoop, calls=%fused_computation.6.clone.1 | loop fusion | bytes 425988 | tf_op jit(solution)/shard_map/while/body/jit(dynamic_index_in_dim)/dynamic_slice | solution.py:127
  38.5 0.9 constant_dynamic-slice_fusion.5
  39.9 1.6 %constant_dynamic-slice_fusion.4 = f32[1,13,4096]{2,0,1:T(1,128)S(1)} fusion(f32[10,13,4096]{2,0,1:T(8,128)} %get-tuple-element.147, s32[]{:T(128)} %get-tuple-element.139), kind=kLoop, calls=%fused_computation.6.clone.1 | loop fusion | bytes 425988 | tf_op jit(solution)/shard_map/while/body/jit(dynamic_index_in_dim)/dynamic_slice | solution.py:127
  41.5 0.9 constant_dynamic-slice_fusion.5
  42.9 1.6 %constant_dynamic-slice_fusion.4 = f32[1,13,4096]{2,0,1:T(1,128)S(1)} fusion(f32[10,13,4096]{2,0,1:T(8,128)} %get-tuple-element.147, s32[]{:T(128)} %get-tuple-element.139), kind=kLoop, calls=%fused_computation.6.clone.1 | loop fusion | bytes 425988 | tf_op jit(solution)/shard_map/while/body/jit(dynamic_index_in_dim)/dynamic_slice | solution.py:127
  44.6 0.9 constant_dynamic-slice_fusion.5
  46.0 1.6 %constant_dynamic-slice_fusion.4 = f32[1,13,4096]{2,0,1:T(1,128)S(1)} fusion(f32[10,13,4096]{2,0,1:T(8,128)} %get-tuple-element.147, s32[]{:T(128)} %get-tuple-element.139), kind=kLoop, calls=%fused_computation.6.clone.1 | loop fusion | bytes 425988 | tf_op jit(solution)/shard_map/while/body/jit(dynamic_index_in_dim)/dynamic_slice | solution.py:127
  47.7 0.9 constant_dynamic-slice_fusion.5
  49.1 1.6 %constant_dynamic-slice_fusion.4 = f32[1,13,4096]{2,0,1:T(1,128)S(1)} fusion(f32[10,13,4096]{2,0,1:T(8,128)} %get-tuple-element.147, s32[]{:T(128)} %get-tuple-element.139), kind=kLoop, calls=%fused_computation.6.clone.1 | loop fusion | bytes 425988 | tf_op jit(solution)/shard_map/while/body/jit(dynamic_index_in_dim)/dynamic_slice | solution.py:127
  50.7 0.9 constant_dynamic-slice_fusion.5
  52.1 1.6 %constant_dynamic-slice_fusion.4 = f32[1,13,4096]{2,0,1:T(1,128)S(1)} fusion(f32[10,13,4096]{2,0,1:T(8,128)} %get-tuple-element.147, s32[]{:T(128)} %get-tuple-element.139), kind=kLoop, calls=%fused_computation.6.clone.1 | loop fusion | bytes 425988 | tf_op jit(solution)/shard_map/while/body/jit(dynamic_index_in_dim)/dynamic_slice | solution.py:127
  53.8 0.9 constant_dynamic-slice_fusion.5
  55.2 1.6 %constant_dynamic-slice_fusion.4 = f32[1,13,4096]{2,0,1:T(1,128)S(1)} fusion(f32[10,13,4096]{2,0,1:T(8,128)} %get-tuple-element.147, s32[]{:T(128)} %get-tuple-element.139), kind=kLoop, calls=%fused_computation.6.clone.1 | loop fusion | bytes 425988 | tf_op jit(solution)/shard_map/while/body/jit(dynamic_index_in_dim)/dynamic_slice | solution.py:127
  56.9 0.9 constant_dynamic-slice_fusion.5
  58.3 1.6 %constant_dynamic-slice_fusion.4 = f32[1,13,4096]{2,0,1:T(1,128)S(1)} fusion(f32[10,13,4096]{2,0,1:T(8,128)} %get-tuple-element.147, s32[]{:T(128)} %get-tuple-element.139), kind=kLoop, calls=%fused_computation.6.clone.1 | loop fusion | bytes 425988 | tf_op jit(solution)/shard_map/while/body/jit(dynamic_index_in_dim)/dynamic_slice | solution.py:127
  59.9 0.9 constant_dynamic-slice_fusion.5
  61.3 1.6 %constant_dynamic-slice_fusion.4 = f32[1,13,4096]{2,0,1:T(1,128)S(1)} fusion(f32[10,13,4096]{2,0,1:T(8,128)} %get-tuple-element.147, s32[]{:T(128)} %get-tuple-element.139), kind=kLoop, calls=%fused_computation.6.clone.1 | loop fusion | bytes 425988 | tf_op jit(solution)/shard_map/while/body/jit(dynamic_index_in_dim)/dynamic_slice | solution.py:127
  63.0 0.9 constant_dynamic-slice_fusion.5
  64.4 30.9 %all-gather.1 = f32[8,13,32]{2,1,0:T(8,128)S(1)} all-gather(f32[1,13,32]{2,1,0:T(8,128)S(1)} %bitcast.71), channel_id=2, replica_groups=mesh['px'=4,'py'=8] {'py'}, dimensions={0}, use_global_device_ids=true | all-gather | bytes 14976 | tf_op jit(solution)/shard_map/all_gather | solution.py:133
  (79 shorter events, 21.0 us)
Async XLA Ops:
  0.6 10.6 %copy-start.1 = (f32[8,8,640]{2,1,0:T(8,128)S(1)}, f32[8,8,640]{2,1,0:T(8,128)}, u32[]{:S(2)}) copy-start(f32[8,8,640]{2,1,0:T(8,128)} %param.9) | copy-start | bytes 491524
  0.6 10.6 %copy-start = (f32[8,8,640]{2,1,0:T(8,128)S(1)}, f32[8,8,640]{2,1,0:T(8,128)}, u32[]{:S(2)}) copy-start(f32[8,8,640]{2,1,0:T(8,128)} %param.10) | copy-start | bytes 491524
  0.7 10.8 %copy-start.4 = (f32[8,8,640]{2,1,0:T(8,128)S(1)}, f32[8,8,640]{2,1,0:T(8,128)}, u32[]{:S(2)}) copy-start(f32[8,8,640]{2,1,0:T(8,128)} %param.11) | copy-start | bytes 491524
  1.6 7.5 %collective-permute-start.1 = (f32[2,2,8,640]{3,2,1,0:T(8,128)S(1)}, f32[2,2,8,640]{3,2,1,0:T(8,128)S(1)}, u32[]{:S(2)}, u32[]{:S(2)}) collective-permute-start(f32[2,2,8,640]{3,2,1,0:T(8,128)S(1)} %get-tuple-element.76), channel_id=1, source_target_pairs={{8,0},{16,8},{24,16},{0,24},{9,1},{17,9},{25,17},{1,25},{10,2},{18... | collective-permute-start | bytes 245768 | tf_op jit(solution)/shard_map/ppermute | solution.py:16
  4.0 5.0 %collective-permute-start = (f32[2,2,8,640]{3,2,1,0:T(8,128)S(1)}, f32[2,2,8,640]{3,2,1,0:T(8,128)S(1)}, u32[]{:S(2)}, u32[]{:S(2)}) collective-permute-start(f32[2,2,8,640]{3,2,1,0:T(8,128)S(1)} %get-tuple-element.77), channel_id=1, source_target_pairs={{0,8},{8,16},{16,24},{24,0},{1,9},{9,17},{17,25},{25,1},{2,10},{10... | collective-permute-start | bytes 245768 | tf_op jit(solution)/shard_map/ppermute | solution.py:15
  11.5 6.0 %collective-permute-start.2 = (f32[2,8,2,640]{3,2,1,0:T(2,128)S(1)}, f32[2,8,2,640]{3,2,1,0:T(2,128)S(1)}, u32[]{:S(2)}, u32[]{:S(2)}) collective-permute-start(f32[2,8,2,640]{3,2,1,0:T(2,128)S(1)} %get-tuple-element.72), channel_id=1, source_target_pairs={{0,1},{1,2},{2,3},{3,4},{4,5},{5,6},{6,7},{8,9},{9,10},{10,11},{11... | collective-permute-start | bytes 245768 | tf_op jit(solution)/shard_map/ppermute | solution.py:15
  14.9 6.7 %collective-permute-start.3 = (f32[2,8,2,640]{3,2,1,0:T(2,128)S(1)}, f32[2,8,2,640]{3,2,1,0:T(2,128)S(1)}, u32[]{:S(2)}, u32[]{:S(2)}) collective-permute-start(f32[2,8,2,640]{3,2,1,0:T(2,128)S(1)} %get-tuple-element.73), channel_id=1, source_target_pairs={{1,0},{2,1},{3,2},{4,3},{5,4},{6,5},{7,6},{9,8},{10,9},{11,10},{12... | collective-permute-start | bytes 245768 | tf_op jit(solution)/shard_map/ppermute | solution.py:16
  16.2 6.2 %copy-start.2 = (f32[8,8,640]{2,1,0:T(8,128)S(1)}, f32[8,8,640]{2,1,0:T(8,128)}, u32[]{:S(2)}) copy-start(f32[8,8,640]{2,1,0:T(8,128)} %param.12) | copy-start | bytes 491524
  21.8 1.0 %copy-start.3 = (s32[8,8,640]{2,1,0:T(8,128)S(1)}, s32[8,8,640]{2,1,0:T(8,128)}, u32[]{:S(2)}) copy-start(s32[8,8,640]{2,1,0:T(8,128)} %param.13) | copy-start | bytes 491524
